TPU v7x, 32 devices: a whole 2x2x4 slice. The times are simulated.
32 devices in a mesh: wide: 8 (over z, x), narrow: 4 (over y, core).
Axes of the slice: x: 2, y: 2, z: 4, core: 2. Of those that a mesh axis runs over, the one named last changes fastest.
Arguments:
- states: bfloat16 [256, 262144], P('narrow', 'wide'), may hold values from -6 to 6
- obs_ens: bfloat16 [256, 32768], P('narrow', 'wide'), may hold values from -6 to 6
- obs_value: float32 [32768], P('wide'), may hold values from -6 to 6
- obs_prec: float32 [32768], P('wide'), may hold values from 0.1 to 1
- obs_pick: int32 [32, 1024], P('wide'), may hold values from 0 to 4607, as said below
- taper: float32 [32, 1024], P(('wide', 'narrow')), may hold values from 0.1 to 1
Outputs:
- analysis: bfloat16 [256, 262144], P('narrow', 'wide')
Inputs may be any that keep to these rules, and one draw needn't show every extreme that they name: `obs_pick`: within a region the 1024 rows are distinct.
All inputs are finite; a program needn't handle non-finite values.
Results may differ from a plain program's by a relative error of at most 0.0057.
Values may be sent and summed in bfloat16 or wider, within the bound.
No kernel may reach another device: no remote copies, remote signals or barrier semaphores. Data moves between devices by JAX's collectives and lax.ppermute only.
A program may use at most 64 MiB of HBM per device.

v0:
```python
import jax
import jax.numpy as jnp
from jax import lax
from jax.sharding import PartitionSpec as P

HALO = 256
ITERS = 6


def padded(array, sides, width):
    for axis, dim in sides:
        size, length = (lax.axis_size(axis), array.shape[dim])
        up = [(i, (i + 1) % size) for i in range(size)]
        down = [(j, i) for i, j in up]
        last = lax.slice_in_dim(array, length - width, length, axis=dim)
        leading = lax.slice_in_dim(array, 0, width, axis=dim)
        before = lax.ppermute(last, axis, up)
        after = lax.ppermute(leading, axis, down)
        array = jnp.concatenate([before, array, after], axis=dim)
    return array


def analyse(ensemble, observed, precision, taper_row, regional):
    members = ensemble.shape[0]
    obs_mean = jnp.mean(ensemble, axis=0)
    obs_pert = ensemble - obs_mean
    obs_weight = precision * taper_row
    scaled = (obs_pert * jnp.sqrt(obs_weight)).astype(jnp.bfloat16)
    identity = jnp.eye(members, dtype=jnp.float32)
    gram_sum = lax.dot_general(
        scaled, scaled, (((1,), (1,)), ((), ())), preferred_element_type=jnp.float32
    )
    precision_matrix = gram_sum + (members - 1.0) * identity
    forcing = jnp.dot(
        obs_pert,
        obs_weight * (observed - obs_mean),
        precision=lax.Precision.HIGHEST,
        preferred_element_type=jnp.float32,
    )
    norm_scale = jnp.sqrt(jnp.sum(precision_matrix * precision_matrix))
    current = precision_matrix / norm_scale
    root_iter = identity
    for iteration in range(ITERS):
        middle = 1.5 * identity - 0.5 * jnp.dot(
            root_iter, current, precision=lax.Precision.HIGHEST, preferred_element_type=jnp.float32
        )
        current = jnp.dot(
            current, middle, precision=lax.Precision.HIGHEST, preferred_element_type=jnp.float32
        )
        root_iter = jnp.dot(
            middle, root_iter, precision=lax.Precision.HIGHEST, preferred_element_type=jnp.float32
        )
    inv_root = root_iter / jnp.sqrt(norm_scale)
    inner = jnp.dot(
        inv_root, forcing, precision=lax.Precision.HIGHEST, preferred_element_type=jnp.float32
    )
    mean_weights = jnp.dot(
        inv_root, inner, precision=lax.Precision.HIGHEST, preferred_element_type=jnp.float32
    )
    transform = (jnp.sqrt(members - 1.0) * inv_root + mean_weights[:, None]).astype(jnp.bfloat16)
    state_mean = jnp.mean(regional.astype(jnp.float32), axis=0)
    state_pert = (regional.astype(jnp.float32) - state_mean).astype(jnp.bfloat16)
    mixed = lax.dot_general(
        transform, state_pert, (((0,), (0,)), ((), ())), preferred_element_type=jnp.float32
    )
    return (state_mean + mixed).astype(jnp.bfloat16)


def body(states, obs_ens, obs_value, obs_prec, obs_pick, taper):
    band_regions = lax.axis_size("narrow")
    position = lax.axis_index("narrow")
    members = obs_ens.shape[0] * band_regions
    extended = padded(obs_ens, (("wide", 1),), HALO)
    stat_pair = padded(jnp.stack([obs_value, obs_prec]), (("wide", 1),), HALO)
    own_rows = lax.dynamic_index_in_dim(obs_pick, position, 0, keepdims=False)
    chosen = jnp.take(extended, obs_pick.reshape(-1), axis=1).reshape(
        extended.shape[0], band_regions, -1
    )
    arrived = lax.all_to_all(chosen, "narrow", split_axis=1, concat_axis=0, tiled=True)
    picked = arrived.reshape(members, -1)
    stat_rows = jnp.take(stat_pair, own_rows, axis=1)
    regional = lax.all_to_all(states, "narrow", split_axis=1, concat_axis=0, tiled=True)
    result = analyse(picked.astype(jnp.float32), stat_rows[0], stat_rows[1], taper[0], regional)
    return lax.all_to_all(result, "narrow", split_axis=0, concat_axis=1, tiled=True)


def solution(mesh):
    return jax.shard_map(
        body,
        mesh=mesh,
        in_specs=(
            P("narrow", "wide"),
            P("narrow", "wide"),
            P("wide"),
            P("wide"),
            P("wide", None),
            P(("wide", "narrow"), None),
        ),
        out_specs=P("narrow", "wide"),
        check_vma=False,
    )
```

profile of v0, /device:TPU:0, one launch (start us, length us, event | category | flops | bytes accessed | tf_op | source)
XLA Modules:
  0.0 160.5 jit_solution(12780005530070920755)
XLA Ops:
  0.0 0.7 pad_maximum_fusion.3
  0.7 3.0 %collective-permute-start.2 = (f32[2,256]{1,0:T(2,128)S(1)}, f32[2,256]{1,0:T(2,128)S(1)}, u32[]{:S(2)}, u32[]{:S(2)}) collective-permute-start(f32[2,256]{1,0:T(2,128)S(1)} %get-tuple-element.11), channel_id=1, source_target_pairs={{0,4},{4,8},{8,12},{12,16},{16,20},{20,24},{24,28},{28,0},{1,5},{5... | collective-permute-start | bytes 6152 | tf_op jit(solution)/shard_map/ppermute | solution.py:17
  3.7 3.1 %collective-permute-start.3 = (f32[2,256]{1,0:T(2,128)S(1)}, f32[2,256]{1,0:T(2,128)S(1)}, u32[]{:S(2)}, u32[]{:S(2)}) collective-permute-start(f32[2,256]{1,0:T(2,128)S(1)} %get-tuple-element.12), channel_id=1, source_target_pairs={{4,0},{8,4},{12,8},{16,12},{20,16},{24,20},{28,24},{0,28},{5,1},{9... | collective-permute-start | bytes 6152 | tf_op jit(solution)/shard_map/ppermute | solution.py:18
  6.9 1.5 copy.24
  8.5 4.7 %collective-permute-start.1 = (bf16[64,256]{0,1:T(8,128)(2,1)S(1)}, bf16[64,256]{0,1:T(8,128)(2,1)S(1)}, u32[]{:S(2)}, u32[]{:S(2)}) collective-permute-start(bf16[64,256]{0,1:T(8,128)(2,1)S(1)} %get-tuple-element.10), channel_id=1, source_target_pairs={{4,0},{8,4},{12,8},{16,12},{20,16},{24,20},{28,24},{0,28},{5,1},{9... | collective-permute-start | bytes 98312 | tf_op jit(solution)/shard_map/ppermute | solution.py:18
  13.9 0.7 compare_select_fusion.2
  14.7 0.7 copy.34
  15.4 0.9 copy.29
  16.4 4.6 %copy.36 = bf16[8,4,8,8192]{3,2,0,1:T(8,128)(2,1)} copy(bf16[8,4,8,8192]{3,2,1,0:T(8,128)(2,1)} %bitcast.95) | data formatting | bytes 8388608 | tf_op jit(solution)/shard_map/all_to_all | solution.py:82
  21.3 12.1 %gather_fusion = bf16[4096,64]{1,0:T(8,128)(2,1)S(1)} fusion(bf16[64,4608]{0,1:T(8,128)(2,1)S(1)} %pad_maximum_fusion, s32[4096]{0:T(1024)S(1)} %broadcast_clamp_fusion), kind=kCustom, calls=%fused_computation | custom fusion | bytes 1064960 | tf_op jit(solution)/shard_map/jit(_take)/gather | solution.py:76
  33.7 0.8 broadcast_select_fusion
  34.6 3.5 %all-to-all-start.1 = ((bf16[64,4,1024]{2,0,1:T(8,128)(2,1)}), bf16[64,4,1024]{2,0,1:T(8,128)(2,1)S(1)}, u32[]{:S(2)}, u32[]{:S(2)}) async-start(bf16[64,4,1024]{2,0,1:T(8,128)(2,1)} %broadcast_select_fusion), calls=%async_computation.1 | async-start | bytes 1048576 | tf_op jit(solution)/shard_map/all_to_all | solution.py:79
  38.9 4.0 %gather_fusion.1 = f32[1024,2]{1,0:T(8,128)} fusion(f32[2,4608]{0,1:T(8,128)S(1)} %copy.28, s32[1024]{0:T(1024)S(1)} %broadcast_clamp_fusion.1), kind=kCustom, calls=%fused_computation.1 | custom fusion | bytes 20480 | tf_op jit(solution)/shard_map/jit(_take)/gather | solution.py:81
  42.9 1.2 select_bitcast_fusion
  44.2 2.7 %all-to-all-done.1 = bf16[64,4,1024]{2,0,1:T(8,128)(2,1)S(1)} async-done(((bf16[64,4,1024]{2,0,1:T(8,128)(2,1)}), bf16[64,4,1024]{2,0,1:T(8,128)(2,1)S(1)}, u32[]{:S(2)}, u32[]{:S(2)}) %all-to-all-start.1) | async-done | bytes 524320 | tf_op jit(solution)/shard_map/all_to_all | solution.py:79
  46.8 5.0 %all-to-all-start = ((bf16[64,4,8192]{2,0,1:T(8,128)(2,1)}), bf16[64,4,8192]{2,0,1:T(8,128)(2,1)}, u32[]{:S(2)}, u32[]{:S(2)}) async-start(bf16[64,4,8192]{2,0,1:T(8,128)(2,1)} %bitcast.92), calls=%async_computation | async-start | bytes 8388608 | tf_op jit(solution)/shard_map/all_to_all | solution.py:82
  52.9 1.0 multiply_reduce_fusion
  61.2 0.9 convolution_bitcast_fusion
  62.7 37.2 %all-to-all-done = bf16[64,4,8192]{2,0,1:T(8,128)(2,1)} async-done(((bf16[64,4,8192]{2,0,1:T(8,128)(2,1)}), bf16[64,4,8192]{2,0,1:T(8,128)(2,1)}, u32[]{:S(2)}, u32[]{:S(2)}) %all-to-all-start) | async-done | bytes 4194336 | tf_op jit(solution)/shard_map/all_to_all | solution.py:82
  99.9 2.9 %convert_reduce_fusion = f32[8192]{0:T(1024)S(1)} fusion(bf16[64,4,8192]{2,0,1:T(8,128)(2,1)} %all-to-all-done), kind=kLoop, calls=%fused_computation.7 | loop fusion | flops 4186112 | bytes 4227072 | tf_op jit(solution)/shard_map/reduce_sum | solution.py:61
  102.8 3.3 %fusion.1 = bf16[256,8192]{1,0:T(8,128)(2,1)S(1)} fusion(f32[8192]{0:T(1024)S(1)} %broadcast_multiply_fusion, bf16[64,4,8192]{2,0,1:T(8,128)(2,1)} %all-to-all-done), kind=kLoop, calls=%fused_computation.5 | loop fusion | flops 6291456 | bytes 8421376 | tf_op jit(solution)/shard_map/convert_element_type | solution.py:62
  106.2 1.4 fusion
  107.5 50.7 %all_to_all.41 = bf16[4,64,8192]{2,1,0:T(8,128)(2,1)S(1)} all-to-all(bf16[4,64,8192]{2,1,0:T(8,128)(2,1)S(1)} %bitcast.91), channel_id=1, replica_groups=mesh['wide'=8,'narrow'=4] {'narrow'}, dimensions={0} | all-to-all | bytes 8388608 | tf_op jit(solution)/shard_map/all_to_all | solution.py:84
  158.2 2.3 %copy.33 = bf16[4,8,8,8192]{3,2,0,1:T(8,128)(2,1)} copy(bf16[4,8,8,8192]{3,2,1,0:T(8,128)(2,1)S(1)} %bitcast.93) | data formatting | bytes 8388608 | tf_op jit(solution)/shard_map/all_to_all | solution.py:84
  (45 shorter events, 10.2 us)
Async XLA Ops:
  0.7 37.3 %collective-permute-start.2 = (f32[2,256]{1,0:T(2,128)S(1)}, f32[2,256]{1,0:T(2,128)S(1)}, u32[]{:S(2)}, u32[]{:S(2)}) collective-permute-start(f32[2,256]{1,0:T(2,128)S(1)} %get-tuple-element.11), channel_id=1, source_target_pairs={{0,4},{4,8},{8,12},{12,16},{16,20},{20,24},{24,28},{28,0},{1,5},{5... | collective-permute-start | bytes 6152 | tf_op jit(solution)/shard_map/ppermute | solution.py:17
  3.7 34.3 %collective-permute-start.3 = (f32[2,256]{1,0:T(2,128)S(1)}, f32[2,256]{1,0:T(2,128)S(1)}, u32[]{:S(2)}, u32[]{:S(2)}) collective-permute-start(f32[2,256]{1,0:T(2,128)S(1)} %get-tuple-element.12), channel_id=1, source_target_pairs={{4,0},{8,4},{12,8},{16,12},{20,16},{24,20},{28,24},{0,28},{5,1},{9... | collective-permute-start | bytes 6152 | tf_op jit(solution)/shard_map/ppermute | solution.py:18
  8.4 12.6 %collective-permute-start = (bf16[64,256]{0,1:T(8,128)(2,1)S(1)}, bf16[64,256]{0,1:T(8,128)(2,1)S(1)}, u32[]{:S(2)}, u32[]{:S(2)}) collective-permute-start(bf16[64,256]{0,1:T(8,128)(2,1)S(1)} %get-tuple-element.9), channel_id=1, source_target_pairs={{0,4},{4,8},{8,12},{12,16},{16,20},{20,24},{24,28},{28,0},{1,5},{5... | collective-permute-start | bytes 98312 | tf_op jit(solution)/shard_map/ppermute | solution.py:17
  8.5 12.5 %collective-permute-start.1 = (bf16[64,256]{0,1:T(8,128)(2,1)S(1)}, bf16[64,256]{0,1:T(8,128)(2,1)S(1)}, u32[]{:S(2)}, u32[]{:S(2)}) collective-permute-start(bf16[64,256]{0,1:T(8,128)(2,1)S(1)} %get-tuple-element.10), channel_id=1, source_target_pairs={{4,0},{8,4},{12,8},{16,12},{20,16},{24,20},{28,24},{0,28},{5,1},{9... | collective-permute-start | bytes 98312 | tf_op jit(solution)/shard_map/ppermute | solution.py:18
  21.2 16.8 %copy-start = (f32[4096]{0:T(1024)S(1)}, f32[4096]{0:T(1024)}, u32[]{:S(2)}) copy-start(f32[4096]{0:T(1024)} %param.9) | copy-start | bytes 49156
  21.3 16.8 %copy-start.1 = (f32[4096]{0:T(1024)S(1)}, f32[4096]{0:T(1024)}, u32[]{:S(2)}) copy-start(f32[4096]{0:T(1024)} %param.8) | copy-start | bytes 49156
  34.6 12.3 %all-to-all-start.1 = ((bf16[64,4,1024]{2,0,1:T(8,128)(2,1)}), bf16[64,4,1024]{2,0,1:T(8,128)(2,1)S(1)}, u32[]{:S(2)}, u32[]{:S(2)}) async-start(bf16[64,4,1024]{2,0,1:T(8,128)(2,1)} %broadcast_select_fusion), calls=%async_computation.1 | async-start | bytes 1048576 | tf_op jit(solution)/shard_map/all_to_all | solution.py:79
  46.8 53.1 %all-to-all-start = ((bf16[64,4,8192]{2,0,1:T(8,128)(2,1)}), bf16[64,4,8192]{2,0,1:T(8,128)(2,1)}, u32[]{:S(2)}, u32[]{:S(2)}) async-start(bf16[64,4,8192]{2,0,1:T(8,128)(2,1)} %bitcast.92), calls=%async_computation | async-start | bytes 8388608 | tf_op jit(solution)/shard_map/all_to_all | solution.py:82
where the time goes:
time: 161 us
  blocking collectives  50.7 us (31%)
  waiting for transfers between devices  39.9 us (25%)
  local copies, waits for them, and re-layouts  27.6 us (17%)
  starting transfers between devices  19.4 us (12%)
  other arithmetic  11.7 us (7%)
  matrix products  10.2 us (6%)
    all_to_all x1, blocking collectives, body(): lax.all_to_all(result, 'narrow', split_axis=0, concat_axis=1, tiled=True)  50.7 us
    all_to_all x1, waiting for transfers between devices, body(): lax.all_to_all(states, 'narrow', split_axis=1, concat_axis=0, tiled=True)  37.2 us
    gather x2, local copies, waits for them, and re-layouts, body(): jnp.take(extended, obs_pick.reshape(-1), axis=1)  12.5 us
    ppermute x2, starting transfers between devices, padded(): after = lax.ppermute(leading, axis, down)  7.81 us
    all_to_all x1, starting transfers between devices, body(): lax.all_to_all(states, 'narrow', split_axis=1, concat_axis=0, tiled=True)  5.04 us
    all_to_all x1, local copies, waits for them, and re-layouts, body(): lax.all_to_all(states, 'narrow', split_axis=1, concat_axis=0, tiled=True)  4.64 us
    gather x1, local copies, waits for them, and re-layouts, body(): stat_rows = jnp.take(stat_pair, own_rows, axis=1)  4.04 us
    all_to_all x1, starting transfers between devices, body(): lax.all_to_all(chosen, 'narrow', split_axis=1, concat_axis=0, tiled=True)  3.47 us
  transfers between devices with their start and end apart: 6, of which 2 were waited for; matrix products, arithmetic and copies ran while one was open for 24% of the time, Pallas kernels for 0%

commit v1 on v0

--- a/solution.py
+++ b/solution.py
@@ -79,7 +79,18 @@
     arrived = lax.all_to_all(chosen, "narrow", split_axis=1, concat_axis=0, tiled=True)
     picked = arrived.reshape(members, -1)
     stat_rows = jnp.take(stat_pair, own_rows, axis=1)
-    regional = lax.all_to_all(states, "narrow", split_axis=1, concat_axis=0, tiled=True)
+    ways, here = (lax.axis_size("narrow"), lax.axis_index("narrow"))
+    width_2 = states.shape[1] // ways
+    lengths = list(states.shape)
+    lengths[1] = width_2
+    height = lengths[0]
+    lengths[0] = height * ways
+    regional = jnp.zeros(lengths, states.dtype)
+    for mask in range(ways):
+        part = lax.dynamic_slice_in_dim(states, (here ^ mask) * width_2, width_2, axis=1)
+        if mask:
+            part = lax.ppermute(part, "narrow", [(d, d ^ mask) for d in range(ways)])
+        regional = lax.dynamic_update_slice_in_dim(regional, part, (here ^ mask) * height, axis=0)
     result = analyse(picked.astype(jnp.float32), stat_rows[0], stat_rows[1], taper[0], regional)
     return lax.all_to_all(result, "narrow", split_axis=0, concat_axis=1, tiled=True)
 

time: 161 us -> 139 us (0.86)
  waiting for transfers between devices: 39.9 us -> 17.9 us
  local copies, waits for them, and re-layouts: 27.6 us -> 33.3 us
  other arithmetic: 11.7 us -> 6.26 us
  starting transfers between devices: 19.4 us -> 16.6 us
  matrix products: 10.2 us -> 12.4 us
    all_to_all x1 -> x0, waiting for transfers between devices: 37.2 us -> none  [body(): lax.all_to_all(states, 'narrow', split_axis=1, concat_axis=0, tiled=True)]
    all_to_all x1, waiting for transfers between devices: 2.69 us -> 16.4 us  [body(): lax.all_to_all(chosen, 'narrow', split_axis=1, concat_axis=0, tiled=True)]
    dynamic_update_slice x0 -> x3, local copies, waits for them, and re-layouts: none -> 6.85 us  [body(): lax.dynamic_update_slice_in_dim(regional, part, (here ^ mask) * height, a...]
    all_to_all x1 -> x0, starting transfers between devices: 5.04 us -> none  [body(): lax.all_to_all(states, 'narrow', split_axis=1, concat_axis=0, tiled=True)]
    all_to_all x1 -> x0, local copies, waits for them, and re-layouts: 4.64 us -> none  [body(): lax.all_to_all(states, 'narrow', split_axis=1, concat_axis=0, tiled=True)]
    convert_element_type x1 -> x0, other arithmetic: 3.35 us -> none  [analyse(): (regional.astype(jnp.float32) - state_mean).astype(jnp.bfloat16)]
    ppermute x0 -> x3, starting transfers between devices: none -> 3.11 us  [body(): part = lax.ppermute(part, 'narrow', [(d, d ^ mask) for d in range(ways)])]
    ppermute x2, starting transfers between devices: 3.07 us -> 0.01 us  [padded(): before = lax.ppermute(last, axis, up)]
  transfers between devices with their start and end apart: 6 -> 8, of which waited for: 2 -> 2; matrix products, arithmetic and copies ran while one was open for 24% -> 25% of each run, Pallas kernels for 0% -> 0%
where the time goes in v1:
time: 139 us
  blocking collectives  51 us (37%)
  local copies, waits for them, and re-layouts  33.3 us (24%)
  waiting for transfers between devices  17.9 us (13%)
  starting transfers between devices  16.6 us (12%)
  matrix products  12.4 us (9%)
  other arithmetic  6.26 us (5%)
    all_to_all x1, blocking collectives, body(): lax.all_to_all(result, 'narrow', split_axis=0, concat_axis=1, tiled=True)  51 us
    all_to_all x1, waiting for transfers between devices, body(): lax.all_to_all(chosen, 'narrow', split_axis=1, concat_axis=0, tiled=True)  16.4 us
    gather x2, local copies, waits for them, and re-layouts, body(): jnp.take(extended, obs_pick.reshape(-1), axis=1)  12.5 us
    ppermute x2, starting transfers between devices, padded(): after = lax.ppermute(leading, axis, down)  9.88 us
    dynamic_update_slice x3, local copies, waits for them, and re-layouts, body(): lax.dynamic_update_slice_in_dim(regional, part, (here ^ mask) * height, a...  6.85 us
    gather x1, local copies, waits for them, and re-layouts, body(): stat_rows = jnp.take(stat_pair, own_rows, axis=1)  4.02 us
    dot_general x1, matrix products, analyse(): lax.dot_general(transform, state_pert, (((0,), (0,)), ((), ())), preferre...  3.66 us
    all_to_all x1, starting transfers between devices, body(): lax.all_to_all(chosen, 'narrow', split_axis=1, concat_axis=0, tiled=True)  3.65 us
  transfers between devices with their start and end apart: 8, of which 2 were waited for; matrix products, arithmetic and copies ran while one was open for 25% of the time, Pallas kernels for 0%

profile of v1, /device:TPU:0, one launch (start us, length us, event | category | flops | bytes accessed | tf_op | source)
XLA Modules:
  0.0 138.7 jit_solution(7686517732266846257)
XLA Ops:
  0.0 2.6 %broadcast_in_dim.28 = bf16[256,8192]{1,0:T(8,128)(2,1)} broadcast(bf16[]{:T(256)} %constant.19.clone.1), dimensions={} | broadcast | bytes 4194306 | tf_op jit(solution)/shard_map/broadcast_in_dim | solution.py:88
  2.6 1.1 copy-done
  3.7 2.2 %constant_dynamic-slice_fusion.1 = (bf16[64,8192]{1,0:T(8,128)(2,1)}, bf16[64,8192]{1,0:T(8,128)(2,1)}, bf16[256,8192]{1,0:T(8,128)(2,1)}, bf16[64,8192]{1,0:T(8,128)(2,1)}) fusion(bf16[64,32768]{1,0:T(8,128)(2,1)S(1)} %copy-done, s32[]{:T(128)S(6)} %select_n.76, s32[]{:T(128)S(6)} %select_n.72, bf16[256,8192]{1,0:T(8,128)(2,1)} %broadcast_in_dim.28, ...), kind=kLoop, calls=%fused_computation.57 | loop fusion | bytes 8388628 | tf_op jit(solution)/shard_map/dynamic_slice | solution.py:90
  6.4 2.5 %collective-permute-start.1 = (bf16[64,8192]{1,0:T(8,128)(2,1)}, bf16[64,8192]{1,0:T(8,128)(2,1)}, u32[]{:S(2)}, u32[]{:S(2)}) collective-permute-start(bf16[64,8192]{1,0:T(8,128)(2,1)} %get-tuple-element.12), channel_id=1, source_target_pairs={{0,2},{1,3},{2,0},{3,1},{4,6},{5,7},{6,4},{7,5},{8,10},{9,11},{10,... | collective-permute-start | bytes 3145736 | tf_op jit(solution)/shard_map/ppermute | solution.py:92
  9.5 4.8 %collective-permute-start.4 = (bf16[64,256]{0,1:T(8,128)(2,1)S(1)}, bf16[64,256]{0,1:T(8,128)(2,1)S(1)}, u32[]{:S(2)}, u32[]{:S(2)}) collective-permute-start(bf16[64,256]{0,1:T(8,128)(2,1)S(1)} %get-tuple-element.14), channel_id=1, source_target_pairs={{4,0},{8,4},{12,8},{16,12},{20,16},{24,20},{28,24},{0,28},{5,1},{9... | collective-permute-start | bytes 98312 | tf_op jit(solution)/shard_map/ppermute | solution.py:18
  14.8 1.5 %collective-permute-done.4 = bf16[64,256]{0,1:T(8,128)(2,1)S(1)} collective-permute-done((bf16[64,256]{0,1:T(8,128)(2,1)S(1)}, bf16[64,256]{0,1:T(8,128)(2,1)S(1)}, u32[]{:S(2)}, u32[]{:S(2)}) %collective-permute-start.4) | collective-permute-done | bytes 32800 | tf_op jit(solution)/shard_map/ppermute | solution.py:18
  16.2 5.1 %collective-permute-start.6 = (f32[2,256]{1,0:T(2,128)S(1)}, f32[2,256]{1,0:T(2,128)S(1)}, u32[]{:S(2)}, u32[]{:S(2)}) collective-permute-start(f32[2,256]{1,0:T(2,128)S(1)} %get-tuple-element.16), channel_id=1, source_target_pairs={{4,0},{8,4},{12,8},{16,12},{20,16},{24,20},{28,24},{0,28},{5,1},{9... | collective-permute-start | bytes 6152 | tf_op jit(solution)/shard_map/ppermute | solution.py:18
  21.5 12.1 %gather_fusion = bf16[4096,64]{1,0:T(8,128)(2,1)S(1)} fusion(bf16[64,4608]{0,1:T(8,128)(2,1)S(1)} %pad_maximum_fusion, s32[4096]{0:T(1024)S(1)} %broadcast_clamp_fusion), kind=kCustom, calls=%fused_computation | custom fusion | bytes 1064960 | tf_op jit(solution)/shard_map/jit(_take)/gather | solution.py:76
  34.0 0.9 broadcast_select_fusion
  34.9 3.6 %all-to-all-start = ((bf16[64,4,1024]{2,0,1:T(8,128)(2,1)}), bf16[64,4,1024]{2,0,1:T(8,128)(2,1)S(1)}, u32[]{:S(2)}, u32[]{:S(2)}) async-start(bf16[64,4,1024]{2,0,1:T(8,128)(2,1)} %broadcast_select_fusion), calls=%async_computation | async-start | bytes 1048576 | tf_op jit(solution)/shard_map/all_to_all | solution.py:79
  38.6 0.7 copy.25
  39.3 4.0 %gather_fusion.1 = f32[1024,2]{1,0:T(8,128)} fusion(f32[2,4608]{0,1:T(8,128)S(1)} %copy.25, s32[1024]{0:T(1024)S(1)} %broadcast_clamp_fusion.1), kind=kCustom, calls=%fused_computation.1 | custom fusion | bytes 20480 | tf_op jit(solution)/shard_map/jit(_take)/gather | solution.py:81
  43.4 1.2 select_bitcast_fusion
  44.6 16.4 %all-to-all-done = bf16[64,4,1024]{2,0,1:T(8,128)(2,1)S(1)} async-done(((bf16[64,4,1024]{2,0,1:T(8,128)(2,1)}), bf16[64,4,1024]{2,0,1:T(8,128)(2,1)S(1)}, u32[]{:S(2)}, u32[]{:S(2)}) %all-to-all-start) | async-done | bytes 524320 | tf_op jit(solution)/shard_map/all_to_all | solution.py:79
  61.3 0.6 fusion.13
  62.1 1.0 multiply_reduce_fusion
  70.3 0.9 convolution_bitcast_fusion
  71.8 2.3 %constant_dynamic-update-slice_fusion.2 = bf16[256,8192]{1,0:T(8,128)(2,1)} fusion(bf16[256,8192]{1,0:T(8,128)(2,1)} %get-tuple-element.11, bf16[64,8192]{1,0:T(8,128)(2,1)} %collective-permute-done, s32[]{:T(128)S(6)} %select_n.73), kind=kLoop, calls=%fused_computation.60 | loop fusion | bytes 2097156 | tf_op jit(solution)/shard_map/dynamic_update_slice | solution.py:93
  74.2 2.3 %constant_dynamic-update-slice_fusion.1 = bf16[256,8192]{1,0:T(8,128)(2,1)} fusion(bf16[256,8192]{1,0:T(8,128)(2,1)} %constant_dynamic-update-slice_fusion.2, bf16[64,8192]{1,0:T(8,128)(2,1)} %collective-permute-done.1, s32[]{:T(128)S(6)} %select_n.75), kind=kLoop, calls=%fused_computation.58 | loop fusion | bytes 2097156 | tf_op jit(solution)/shard_map/dynamic_update_slice | solution.py:93
  76.4 2.3 %constant_dynamic-update-slice_fusion = bf16[256,8192]{1,0:T(8,128)(2,1)} fusion(bf16[256,8192]{1,0:T(8,128)(2,1)} %constant_dynamic-update-slice_fusion.1, bf16[64,8192]{1,0:T(8,128)(2,1)} %collective-permute-done.2, s32[]{:T(128)S(6)} %select_n.77), kind=kLoop, calls=%fused_computation.56 | loop fusion | bytes 2097156 | tf_op jit(solution)/shard_map/dynamic_update_slice | solution.py:93
  78.7 2.9 %convert_reduce_fusion = f32[8192]{0:T(1024)S(1)} fusion(bf16[256,8192]{1,0:T(8,128)(2,1)} %constant_dynamic-update-slice_fusion), kind=kLoop, calls=%fused_computation.4 | loop fusion | flops 4186112 | bytes 4227072 | tf_op jit(solution)/shard_map/reduce_sum | solution.py:61
  81.6 3.7 %fusion = bf16[256,8192]{1,0:T(8,128)(2,1)S(1)} fusion(bf16[256,8192]{1,0:T(8,128)(2,1)} %constant_dynamic-update-slice_fusion, f32[8192]{0:T(1024)S(1)} %broadcast_multiply_fusion, f32[256,256]{1,0:T(8,128)S(1)} %convolution_divide_fusion, f32[256]{0:T(256)S(1)} %bitcast.96), kind=kOutput, calls=%fused_computation.5 | convolution fusion | flops 1084424192 | bytes 8684544 | tf_op jit(solution)/shard_map/dot_general | solution.py:63
  85.3 51.0 %all_to_all.28 = bf16[4,64,8192]{2,1,0:T(8,128)(2,1)S(1)} all-to-all(bf16[4,64,8192]{2,1,0:T(8,128)(2,1)S(1)} %bitcast.80), channel_id=1, replica_groups=mesh['wide'=8,'narrow'=4] {'narrow'}, dimensions={0} | all-to-all | bytes 8388608 | tf_op jit(solution)/shard_map/all_to_all | solution.py:95
  136.2 2.5 %copy.29 = bf16[4,8,8,8192]{3,2,0,1:T(8,128)(2,1)} copy(bf16[4,8,8,8192]{3,2,1,0:T(8,128)(2,1)S(1)} %bitcast.81) | data formatting | bytes 8388608 | tf_op jit(solution)/shard_map/all_to_all | solution.py:95
  (60 shorter events, 9.5 us)
Async XLA Ops:
  0.0 3.7 %copy-start = (bf16[64,32768]{1,0:T(8,128)(2,1)S(1)}, bf16[64,32768]{1,0:T(8,128)(2,1)}, u32[]{:S(2)}) copy-start(bf16[64,32768]{1,0:T(8,128)(2,1)} %param.6) | copy-start | bytes 12582916
  3.7 5.3 %copy-start.1 = (bf16[64,4096]{1,0:T(8,128)(2,1)S(1)}, bf16[64,4096]{1,0:T(8,128)(2,1)}, u32[]{:S(2)}) copy-start(bf16[64,4096]{1,0:T(8,128)(2,1)} %param.7) | copy-start | bytes 1572868
  3.7 10.6 %copy-start.2 = (s32[4,1024]{1,0:T(4,128)S(1)}, s32[4,1024]{1,0:T(4,128)}, u32[]{:S(2)}) copy-start(s32[4,1024]{1,0:T(4,128)} %param.10) | copy-start | bytes 49156
  3.7 10.7 %copy-start.3 = (f32[4096]{0:T(1024)S(1)}, f32[4096]{0:T(1024)}, u32[]{:S(2)}) copy-start(f32[4096]{0:T(1024)} %param.9) | copy-start | bytes 49156
  3.7 10.8 %copy-start.4 = (f32[4096]{0:T(1024)S(1)}, f32[4096]{0:T(1024)}, u32[]{:S(2)}) copy-start(f32[4096]{0:T(1024)} %param.8) | copy-start | bytes 49156
  3.7 10.8 %copy-start.5 = (f32[1,1024]{1,0:T(1,128)S(1)}, f32[1,1024]{1,0:T(1,128)}, u32[]{:S(2)}) copy-start(f32[1,1024]{1,0:T(1,128)} %param.11) | copy-start | bytes 12292
  5.9 65.9 %collective-permute-start = (bf16[64,8192]{1,0:T(8,128)(2,1)}, bf16[64,8192]{1,0:T(8,128)(2,1)}, u32[]{:S(2)}, u32[]{:S(2)}) collective-permute-start(bf16[64,8192]{1,0:T(8,128)(2,1)} %get-tuple-element.10), channel_id=1, source_target_pairs={{0,1},{1,0},{2,3},{3,2},{4,5},{5,4},{6,7},{7,6},{8,9},{9,8},{10,11... | collective-permute-start | bytes 3145736 | tf_op jit(solution)/shard_map/ppermute | solution.py:92
  6.4 67.8 %collective-permute-start.1 = (bf16[64,8192]{1,0:T(8,128)(2,1)}, bf16[64,8192]{1,0:T(8,128)(2,1)}, u32[]{:S(2)}, u32[]{:S(2)}) collective-permute-start(bf16[64,8192]{1,0:T(8,128)(2,1)} %get-tuple-element.12), channel_id=1, source_target_pairs={{0,2},{1,3},{2,0},{3,1},{4,6},{5,7},{6,4},{7,5},{8,10},{9,11},{10,... | collective-permute-start | bytes 3145736 | tf_op jit(solution)/shard_map/ppermute | solution.py:92
  8.9 67.5 %collective-permute-start.2 = (bf16[64,8192]{1,0:T(8,128)(2,1)}, bf16[64,8192]{1,0:T(8,128)(2,1)}, u32[]{:S(2)}, u32[]{:S(2)}) collective-permute-start(bf16[64,8192]{1,0:T(8,128)(2,1)} %get-tuple-element.9), channel_id=1, source_target_pairs={{0,3},{1,2},{2,1},{3,0},{4,7},{5,6},{6,5},{7,4},{8,11},{9,10},{10,... | collective-permute-start | bytes 3145736 | tf_op jit(solution)/shard_map/ppermute | solution.py:92
  9.5 6.7 %collective-permute-start.4 = (bf16[64,256]{0,1:T(8,128)(2,1)S(1)}, bf16[64,256]{0,1:T(8,128)(2,1)S(1)}, u32[]{:S(2)}, u32[]{:S(2)}) collective-permute-start(bf16[64,256]{0,1:T(8,128)(2,1)S(1)} %get-tuple-element.14), channel_id=1, source_target_pairs={{4,0},{8,4},{12,8},{16,12},{20,16},{24,20},{28,24},{0,28},{5,1},{9... | collective-permute-start | bytes 98312 | tf_op jit(solution)/shard_map/ppermute | solution.py:18
  14.3 7.0 %collective-permute-start.3 = (bf16[64,256]{0,1:T(8,128)(2,1)S(1)}, bf16[64,256]{0,1:T(8,128)(2,1)S(1)}, u32[]{:S(2)}, u32[]{:S(2)}) collective-permute-start(bf16[64,256]{0,1:T(8,128)(2,1)S(1)} %get-tuple-element.13), channel_id=1, source_target_pairs={{0,4},{4,8},{8,12},{12,16},{16,20},{20,24},{24,28},{28,0},{1,5},{5... | collective-permute-start | bytes 98312 | tf_op jit(solution)/shard_map/ppermute | solution.py:17
  16.2 22.3 %collective-permute-start.6 = (f32[2,256]{1,0:T(2,128)S(1)}, f32[2,256]{1,0:T(2,128)S(1)}, u32[]{:S(2)}, u32[]{:S(2)}) collective-permute-start(f32[2,256]{1,0:T(2,128)S(1)} %get-tuple-element.16), channel_id=1, source_target_pairs={{4,0},{8,4},{12,8},{16,12},{20,16},{24,20},{28,24},{0,28},{5,1},{9... | collective-permute-start | bytes 6152 | tf_op jit(solution)/shard_map/ppermute | solution.py:18
  21.3 17.3 %collective-permute-start.5 = (f32[2,256]{1,0:T(2,128)S(1)}, f32[2,256]{1,0:T(2,128)S(1)}, u32[]{:S(2)}, u32[]{:S(2)}) collective-permute-start(f32[2,256]{1,0:T(2,128)S(1)} %get-tuple-element.15), channel_id=1, source_target_pairs={{0,4},{4,8},{8,12},{12,16},{16,20},{20,24},{24,28},{28,0},{1,5},{5... | collective-permute-start | bytes 6152 | tf_op jit(solution)/shard_map/ppermute | solution.py:17
  34.9 26.1 %all-to-all-start = ((bf16[64,4,1024]{2,0,1:T(8,128)(2,1)}), bf16[64,4,1024]{2,0,1:T(8,128)(2,1)S(1)}, u32[]{:S(2)}, u32[]{:S(2)}) async-start(bf16[64,4,1024]{2,0,1:T(8,128)(2,1)} %broadcast_select_fusion), calls=%async_computation | async-start | bytes 1048576 | tf_op jit(solution)/shard_map/all_to_all | solution.py:79
